TPU v7x, 32 devices: a whole 2x2x4 slice. The times are simulated.
32 devices in a mesh: gx: 4 (over z), gy: 4 (over x, core), gz: 2 (over y).
Axes of the slice: x: 2, y: 2, z: 4, core: 2. Of those that a mesh axis runs over, the one named last changes fastest.
Arguments:
- activations: bfloat16 [1024, 8192], P('gy', 'gx'), may hold values from -0.5 to 0.5
- cotangent: bfloat16 [1024, 8192], P('gy', 'gx'), may hold values from -1.5 to 1.5
- gate_pre: bfloat16 [1024, 26624], P('gx', ('gy', 'gz')), may hold values from -6 to 6
- up_pre: bfloat16 [1024, 26624], P('gx', ('gy', 'gz')), may hold values from -6 to 6
- gate_weight: bfloat16 [8192, 26624], P('gx', ('gy', 'gz')), may hold values from -0.0625 to 0.0625
- up_weight: bfloat16 [8192, 26624], P('gx', ('gy', 'gz')), may hold values from -0.0625 to 0.0625
- down_weight: bfloat16 [26624, 8192], P(('gy', 'gz'), 'gx'), may hold values from -0.15625 to 0.15625
Outputs:
- input_grad: bfloat16 [1024, 8192], P('gy', 'gx')
- gate_grad: bfloat16 [8192, 26624], P('gx', ('gy', 'gz'))
- up_grad: bfloat16 [8192, 26624], P('gx', ('gy', 'gz'))
- down_grad: bfloat16 [26624, 8192], P(('gy', 'gz'), 'gx')
All inputs are finite; a program needn't handle non-finite values.
Results may differ from a plain program's by a relative error of at most 0.015.
Values may be sent and summed in bfloat16 or wider, within the bound.
A program may use at most 192 MiB of HBM per device.

v0:
```python
import jax
import jax.numpy as jnp
from jax import lax
from jax.sharding import PartitionSpec as P

over_rows = (((0,), (0,)), ((), ()))
over_cols = (((1,), (1,)), ((), ()))


def swiglu_grads(gate_in, up_in, grad_hidden):
    gate_val = gate_in.astype(jnp.float32)
    up_val = up_in.astype(jnp.float32)
    sigmoid = jax.nn.sigmoid(gate_val)
    hidden = (gate_val * sigmoid * up_val).astype(jnp.bfloat16)
    grad_gate = (grad_hidden * up_val * sigmoid * (1.0 + gate_val * (1.0 - sigmoid))).astype(
        jnp.bfloat16
    )
    grad_up = (grad_hidden * gate_val * sigmoid).astype(jnp.bfloat16)
    return (hidden, grad_gate, grad_up)


def input_terms(grad_gate, grad_up, gate_weight, up_weight):

    def compute(offset, amount):
        total = lax.dot_general(
            grad_gate, gate_weight, over_cols, preferred_element_type=jnp.float32
        )
        return total + lax.dot_general(
            grad_up, up_weight, over_cols, preferred_element_type=jnp.float32
        )

    return compute


def shards(activations, cotangent, gate_pre, up_pre, gate_weight, up_weight, down_weight):
    cotangent_all = lax.all_gather(cotangent, "gy", axis=0, tiled=True)
    gate_all, up_all = (
        lax.all_gather(gate_pre, "gx", axis=0, tiled=True),
        lax.all_gather(up_pre, "gx", axis=0, tiled=True),
    )
    local_sum = lax.dot_general(
        cotangent_all, down_weight, over_cols, preferred_element_type=jnp.float32
    )
    grad_hidden = lax.psum(local_sum, "gx")
    hidden, grad_gate, grad_up = swiglu_grads(gate_all, up_all, grad_hidden)
    down_grad = lax.dot_general(
        hidden, cotangent_all, over_rows, preferred_element_type=jnp.float32
    ).astype(jnp.bfloat16)
    segment = lax.all_gather(activations, "gy", axis=0, tiled=True)
    first = lax.dot_general(segment, grad_gate, over_rows, preferred_element_type=jnp.float32)
    second = lax.dot_general(segment, grad_up, over_rows, preferred_element_type=jnp.float32)
    row_count = activations.shape[0]
    terms = input_terms(grad_gate, grad_up, gate_weight, up_weight)
    share_rows = row_count // lax.axis_size("gz")
    input_share = lax.psum_scatter(
        terms(jnp.int32(0), lax.axis_size(("gy", "gz")) * share_rows),
        ("gy", "gz"),
        scatter_dimension=0,
        tiled=True,
    )
    input_grad = lax.all_gather(input_share.astype(jnp.bfloat16), "gz", axis=0, tiled=True)
    return (input_grad, first.astype(jnp.bfloat16), second.astype(jnp.bfloat16), down_grad)


def solution(mesh):
    in_specs = (
        P("gy", "gx"),
        P("gy", "gx"),
        P("gx", ("gy", "gz")),
        P("gx", ("gy", "gz")),
        P("gx", ("gy", "gz")),
        P("gx", ("gy", "gz")),
        P(("gy", "gz"), "gx"),
    )
    out_specs = (P("gy", "gx"), P("gx", ("gy", "gz")), P("gx", ("gy", "gz")), P(("gy", "gz"), "gx"))
    return jax.shard_map(shards, mesh=mesh, in_specs=in_specs, out_specs=out_specs, check_vma=False)
```

profile of v0, /device:TPU:0, one launch (start us, length us, event | category | flops | bytes accessed | tf_op | source)
XLA Modules:
  0.0 951.3 jit_solution(15693381875679629747)
XLA Ops:
  7.2 0.0 all-gather.6.cloned.1.call-start
  7.2 0.7 all-gather.6.cloned.1.call-update
  7.9 0.0 all-gather.10.cloned.1.call-start
  7.9 0.7 all-gather.10.cloned.1.call-update
  8.6 0.0 all-gather.8.cloned.1.call-start
  8.7 0.7 all-gather.8.cloned.1.call-update
  9.4 0.0 all-reduce.2.cloned.1.call-start
  9.4 37.3 %all-gather.6.cloned.1.call-done = bf16[1024,2048]{1,0:T(8,128)(2,1)} async-done(((bf16[256,2048]{1,0:T(8,128)(2,1)}), bf16[1024,2048]{1,0:T(8,128)(2,1)}) %all-gather.6.cloned.1.call-update) | async-done | bytes 4194320 | tf_op jit(solution)/shard_map/all_gather | solution.py:36
  46.8 22.5 %fusion.17 = f32[1024,3328]{1,0:T(8,128)} fusion(bf16[1024,2048]{1,0:T(8,128)(2,1)} %all-gather.6.cloned.1.call-done, bf16[3328,2048]{1,0:T(8,128)(2,1)} %param.13), kind=kOutput, calls=%fused_computation.24 | convolution fusion | flops 13958643712 | bytes 31457280 | tf_op jit(solution)/shard_map/dot_general | solution.py:41
  69.3 0.0 all-reduce.2.cloned.1.call-update
  69.3 0.0 all-gather.14.cloned.1.call-start
  69.4 0.5 all-gather.14.cloned.1.call-update
  69.9 0.2 reduce-scatter.2.cloned.1.call-start
  70.2 102.1 %all-gather.10.cloned.1.call-done = bf16[1024,3328]{1,0:T(8,128)(2,1)} async-done(((bf16[256,3328]{1,0:T(8,128)(2,1)}), bf16[1024,3328]{1,0:T(8,128)(2,1)}) %all-gather.10.cloned.1.call-update) | async-done | bytes 6815760 | tf_op jit(solution)/shard_map/all_gather | solution.py:38
  172.3 123.8 %all-gather.8.cloned.1.call-done = bf16[1024,3328]{1,0:T(8,128)(2,1)} async-done(((bf16[256,3328]{1,0:T(8,128)(2,1)}), bf16[1024,3328]{1,0:T(8,128)(2,1)}) %all-gather.8.cloned.1.call-update) | async-done | bytes 6815760 | tf_op jit(solution)/shard_map/all_gather | solution.py:39
  296.1 461.1 %all-reduce.2.cloned.1.call-done = f32[1024,3328]{1,0:T(8,128)} async-done(((f32[1024,3328]{1,0:T(8,128)}), f32[1024,3328]{1,0:T(8,128)}) %all-reduce.2.cloned.1.call-update) | async-done | bytes 13631504 | tf_op jit(solution)/shard_map/psum | solution.py:44
  757.1 12.2 %fusion.2 = bf16[1024,3328]{1,0:T(8,128)(2,1)S(1)} fusion(f32[1024,3328]{1,0:T(8,128)} %all-reduce.2.cloned.1.call-done, bf16[1024,3328]{1,0:T(8,128)(2,1)} %all-gather.8.cloned.1.call-done, bf16[1024,3328]{1,0:T(8,128)(2,1)} %all-gather.10.cloned.1.call-done), kind=kLoop, calls=%fused_computation.11 | loop fusion | flops 40894464 | bytes 34078720 | tf_op jit(solution)/shard_map/convert_element_type | solution.py:15
  769.3 0.0 copy-start
  769.3 2.9 copy-done
  772.2 18.1 %fusion.18 = f32[1024,2048]{1,0:T(8,128)} fusion(bf16[1024,3328]{1,0:T(8,128)(2,1)S(1)} %fusion.2, bf16[2048,3328]{1,0:T(8,128)(2,1)} %param.11), kind=kOutput, calls=%fused_computation.25 | convolution fusion | flops 13958643712 | bytes 28835840 | tf_op jit(solution)/shard_map/dot_general | solution.py:25
  790.3 24.1 %convolution_add_fusion = f32[1024,2048]{1,0:T(8,128)} fusion(f32[1024,2048]{1,0:T(8,128)} %fusion.18, bf16[2048,3328]{1,0:T(8,128)(2,1)} %param.12, f32[1024,3328]{1,0:T(8,128)} %all-reduce.2.cloned.1.call-done, bf16[1024,3328]{1,0:T(8,128)(2,1)} %all-gather.10.cloned.1.call-done), kind=kOutput, calls=%fused_computation.22 | convolution fusion | flops 13984595968 | bytes 50855936 | tf_op jit(solution)/shard_map/dot_general | solution.py:28
  814.4 0.0 reduce-scatter.2.cloned.1.call-update
  814.4 0.3 all-gather.12.cloned.1.call-start
  814.7 23.9 %convolution_convert_fusion = bf16[3328,2048]{1,0:T(8,128)(2,1)} fusion(bf16[1024,2048]{1,0:T(8,128)(2,1)} %all-gather.6.cloned.1.call-done, bf16[1024,3328]{1,0:T(8,128)(2,1)} %all-gather.8.cloned.1.call-done, bf16[1024,3328]{1,0:T(8,128)(2,1)} %all-gather.10.cloned.1.call-done), kind=kOutput, calls=%fused_computation.6 | convolution fusion | flops 13992722432 | bytes 31457280 | tf_op jit(solution)/shard_map/dot_general | solution.py:46
  838.6 23.5 %fusion.11 = bf16[2048,3328]{0,1:T(8,128)(2,1)} fusion(bf16[1024,2048]{1,0:T(8,128)(2,1)} %all-gather.14.cloned.1.call-done, f32[1024,3328]{1,0:T(8,128)} %all-reduce.2.cloned.1.call-done, bf16[1024,3328]{1,0:T(8,128)(2,1)} %all-gather.10.cloned.1.call-done), kind=kOutput, calls=%fused_computation.20 | convolution fusion | flops 13989314560 | bytes 38273024 | tf_op jit(solution)/shard_map/dot_general | solution.py:51
  862.1 22.0 %reduce-scatter.2.cloned.1.call-done = f32[128,2048]{1,0:T(8,128)} async-done(((f32[1024,2048]{1,0:T(8,128)}), f32[128,2048]{1,0:T(8,128)}) %reduce-scatter.2.cloned.1.call-update) | async-done | bytes 1048592 | tf_op jit(solution)/shard_map/reduce_scatter | solution.py:55
  884.1 2.1 convert_element_type.37
  886.2 0.0 all-gather.12.cloned.1.call-update
  886.2 21.0 %fusion.10 = bf16[2048,3328]{0,1:T(8,128)(2,1)} fusion(bf16[1024,3328]{1,0:T(8,128)(2,1)} %copy-done, bf16[1024,2048]{1,0:T(8,128)(2,1)} %all-gather.14.cloned.1.call-done), kind=kOutput, calls=%fused_computation.19 | convolution fusion | flops 13965459456 | bytes 24641536 | tf_op jit(solution)/shard_map/dot_general | solution.py:50
  907.3 17.4 %copy.11 = bf16[2048,3328]{1,0:T(8,128)(2,1)} copy(bf16[2048,3328]{0,1:T(8,128)(2,1)} %fusion.10) | data formatting | bytes 27262976
  924.7 17.4 %copy.12 = bf16[2048,3328]{1,0:T(8,128)(2,1)} copy(bf16[2048,3328]{0,1:T(8,128)(2,1)} %fusion.11) | data formatting | bytes 27262976
  942.2 2.3 copy.15
  (2 shorter events, 0.0 us)
Async XLA Ops:
  7.2 39.6 %all-gather.6.cloned.1.call-start = ((), (), s32[]{:S(2)}) async-start(), calls=%async_computation.1 | async-start | bytes 5242880 | tf_op jit(solution)/shard_map/all_gather | solution.py:36
  7.9 164.4 %all-gather.10.cloned.1.call-start = ((), (), s32[]{:S(2)}) async-start(), calls=%async_computation.4 | async-start | bytes 8519680 | tf_op jit(solution)/shard_map/all_gather | solution.py:38
  8.6 287.4 %all-gather.8.cloned.1.call-start = ((), (), s32[]{:S(2)}) async-start(), calls=%async_computation.3 | async-start | bytes 8519680 | tf_op jit(solution)/shard_map/all_gather | solution.py:39
  9.4 747.8 %all-reduce.2.cloned.1.call-start = ((), (), s32[]{:S(2)}) async-start(), calls=%async_computation.2 | async-start | bytes 27262976 | tf_op jit(solution)/shard_map/psum | solution.py:44
  69.3 769.3 %all-gather.14.cloned.1.call-start = ((), (), s32[]{:S(2)}) async-start(), calls=%async_computation.7 | async-start | bytes 5242880 | tf_op jit(solution)/shard_map/all_gather | solution.py:49
  69.9 814.2 %reduce-scatter.2.cloned.1.call-start = ((), (), s32[]{:S(2)}) async-start(), calls=%async_computation.5 | async-start | bytes 9437184 | tf_op jit(solution)/shard_map/reduce_scatter | solution.py:55
  769.3 2.9 copy-start
  814.4 127.7 %all-gather.12.cloned.1.call-start = ((), (), s32[]{:S(2)}) async-start(), calls=%async_computation.6 | async-start | bytes 1572864 | tf_op jit(solution)/shard_map/all_gather | solution.py:61
Sparse Core Ops, SparseCore 0:
  9.6 37.1 all-gather.5
  48.3 123.9 all-gather.9
  173.9 122.1 all-gather.7
  299.0 458.1 all-reduce.1
  758.6 33.3 all-gather.13
  814.6 69.5 reduce-scatter.1
  886.4 21.2 all-gather.11
where the time goes:
time: 952 us; the launch traced here: 951 us
  waiting for transfers between devices  749 us (79%)
  matrix products  133 us (14%)
  local copies, waits for them, and re-layouts  40.1 us (4%)
  other arithmetic  14.3 us (2%)
  between operations  14.1 us (1%)
    psum x1, waiting for transfers between devices, shards(): grad_hidden = lax.psum(local_sum, 'gx')  461 us
    all_gather x1, waiting for transfers between devices, shards(): lax.all_gather(up_pre, 'gx', axis=0, tiled=True)  124 us
    all_gather x1, waiting for transfers between devices, shards(): lax.all_gather(gate_pre, 'gx', axis=0, tiled=True)  102 us
    unnamed x5, local copies, waits for them, and re-layouts  40.1 us
    all_gather x1, waiting for transfers between devices, shards(): cotangent_all = lax.all_gather(cotangent, 'gy', axis=0, tiled=True)  37.3 us
    dot_general x1, matrix products, compute(): lax.dot_general(grad_up, up_weight, over_cols, preferred_element_type=jnp...  24.1 us
    dot_general x1, matrix products, shards(): lax.dot_general(hidden, cotangent_all, over_rows, preferred_element_type=...  23.9 us
    dot_general x1, matrix products, shards(): lax.dot_general(segment, grad_up, over_rows, preferred_element_type=jnp.f...  23.5 us
  transfers between devices with their start and end apart: 7, of which 5 were waited for; matrix products, arithmetic and copies ran while one was open for 19% of the time, Pallas kernels for 0%

commit v1 on v0

v1 whole, which is shorter than its diff:
```python
import jax
import jax.numpy as jnp
from jax import lax
from jax.sharding import PartitionSpec as P

over_rows = (((0,), (0,)), ((), ()))
over_cols = (((1,), (1,)), ((), ()))
BF = jnp.bfloat16
F32 = jnp.float32


def swiglu_grads(gate_in, up_in, grad_hidden):
    gate_val = gate_in.astype(F32)
    up_val = up_in.astype(F32)
    grad_hidden = grad_hidden.astype(F32)
    sigmoid = jax.nn.sigmoid(gate_val)
    hidden = (gate_val * sigmoid * up_val).astype(BF)
    grad_gate = (grad_hidden * up_val * sigmoid * (1.0 + gate_val * (1.0 - sigmoid))).astype(BF)
    grad_up = (grad_hidden * gate_val * sigmoid).astype(BF)
    return hidden, grad_gate, grad_up


def after(value, earlier):
    seen = earlier.reshape(-1)[0].astype(F32)
    return value + jnp.minimum(jnp.abs(seen), 0.0).astype(value.dtype)


def line_gather(block, axis, n):
    me = lax.axis_index(axis)
    right, left = {}, {}
    from_left = from_right = block
    for s in range(1, n):
        from_left = lax.ppermute(from_left, axis, [(i, i + 1) for i in range(s - 1, n - 1)])
        from_right = lax.ppermute(from_right, axis, [(i, i - 1) for i in range(1, n - s + 1)])
        right[s], left[s] = from_left, from_right
    return [block] + [jnp.where(me >= r, right[r], left[n - r]) for r in range(1, n)]


def line_scatter(part, axis, n):
    right = left = None
    for t in range(1, n):
        to_right, to_left = part(n - t), part(t)
        if right is not None:
            to_right = to_right + right.astype(F32)
            to_left = to_left + left.astype(F32)
        right = lax.ppermute(
            to_right.astype(BF), axis, [(i, i + 1) for i in range(min(t, n - 1))]
        )
        left = lax.ppermute(
            to_left.astype(BF), axis, [(i, i - 1) for i in range(max(n - t, 1), n)]
        )
    total = part(0)
    if right is not None:
        total = total + right.astype(F32) + left.astype(F32)
    return total


def pair_scatter(total, axis, n):
    me = lax.axis_index(axis)
    if n & (n - 1):
        return lax.psum_scatter(total, axis, scatter_dimension=0, tiled=False)
    stride = 1
    while stride < n:
        pairs = total.reshape((total.shape[0] // 2, 2) + total.shape[1:])
        bit = (me // stride) % 2
        mine = lax.dynamic_index_in_dim(pairs, bit, 1, keepdims=False)
        theirs = lax.dynamic_index_in_dim(pairs, 1 - bit, 1, keepdims=False)
        got = lax.ppermute(theirs.astype(BF), axis, [(i, i ^ stride) for i in range(n)])
        total = mine + got.astype(F32)
        stride *= 2
    return total[0]


def chunks_of(width):
    tile = 256 if width % 256 == 0 else 64
    units = width // tile
    if width < 2048:
        return [(0, width)]
    sizes = [(units * 5 + 6) // 13, (units * 5 + 6) // 13]
    sizes.append(units - sum(sizes))
    out, at = [], 0
    for size in sizes:
        out.append((at * tile, size * tile))
        at += size
    return out


def shards(activations, cotangent, gate_pre, up_pre, gate_weight, up_weight, down_weight):
    n, ny, nz = lax.axis_size("gx"), lax.axis_size("gy"), lax.axis_size("gz")
    me = lax.axis_index("gx")
    rows = gate_pre.shape[0]
    tokens = n * rows
    width = gate_pre.shape[1]
    feats = activations.shape[1]
    cotangent_all = lax.all_gather(cotangent, "gy", axis=0, tiled=True)
    activations_all = lax.all_gather(activations, "gy", axis=0, tiled=True)

    def relative(whole):
        blocks = whole.reshape(n, rows, whole.shape[1])
        return jnp.concatenate(
            [
                lax.dynamic_index_in_dim(blocks, lax.rem(me - r + n, n), 0, keepdims=False)
                for r in range(n)
            ],
            axis=0,
        )

    cot = relative(cotangent_all)
    act = relative(activations_all)
    total = None
    gate_grad = jnp.zeros((feats, width), BF)
    up_grad = jnp.zeros((feats, width), BF)
    down_grad = jnp.zeros((width, feats), BF)
    chunks = chunks_of(width)
    partials = [
        lax.dot_general(
            cot, lax.slice_in_dim(down_weight, at, at + size, axis=0), over_cols,
            preferred_element_type=F32,
        ).reshape(n, rows, size)
        for at, size in chunks
    ]
    gates, sums = [], []
    for k, (at, size) in enumerate(chunks):
        gate = lax.slice_in_dim(gate_pre, at, at + size, axis=1)
        up = lax.slice_in_dim(up_pre, at, at + size, axis=1)
        if k == 1:
            gate, up = after(gate, partials[1]), after(up, partials[1])
        if k >= 2:
            gate, up = after(gate, sums[k - 2]), after(up, sums[k - 2])
        gates.append((line_gather(gate, "gx", n), line_gather(up, "gx", n)))

        def part(r, k=k):
            term = partials[k][(n - r) % n]
            return after(term, sums[k - 1]) if k and r in (1, n - 1) else term

        sums.append(line_scatter(part, "gx", n).astype(BF))
    for (at, size), (gate, up), own in zip(chunks, gates, sums):
        grad_hidden = line_gather(own, "gx", n)
        done = [swiglu_grads(*terms) for terms in zip(gate, up, grad_hidden)]
        hidden, grad_gate, grad_up = (jnp.concatenate(part, axis=0) for part in zip(*done))
        term = lax.dot_general(
            grad_gate, lax.slice_in_dim(gate_weight, at, at + size, axis=1), over_cols,
            preferred_element_type=F32,
        ) + lax.dot_general(
            grad_up, lax.slice_in_dim(up_weight, at, at + size, axis=1), over_cols,
            preferred_element_type=F32,
        )
        total = term if total is None else total + term
        down = lax.dot_general(hidden, cot, over_rows, preferred_element_type=F32).astype(BF)
        first = lax.dot_general(act, grad_gate, over_rows, preferred_element_type=F32).astype(BF)
        second = lax.dot_general(act, grad_up, over_rows, preferred_element_type=F32).astype(BF)
        down_grad = lax.dynamic_update_slice(down_grad, down, (at, 0))
        gate_grad = lax.dynamic_update_slice(gate_grad, first, (0, at))
        up_grad = lax.dynamic_update_slice(up_grad, second, (0, at))
    total = total.reshape(n, rows, feats)
    total = jnp.stack(
        [lax.dynamic_index_in_dim(total, lax.rem(me - j + n, n), 0, keepdims=False) for j in range(n)]
    ).reshape(ny, tokens // ny, feats)
    share = pair_scatter(total, "gy", ny)
    if nz == 2:
        share = share + lax.ppermute(share.astype(BF), "gz", [(0, 1), (1, 0)]).astype(F32)
        input_grad = share.astype(BF)
    else:
        input_grad = lax.psum(share, "gz").astype(BF)
    return input_grad, gate_grad, up_grad, down_grad


def solution(mesh):
    in_specs = (
        P("gy", "gx"),
        P("gy", "gx"),
        P("gx", ("gy", "gz")),
        P("gx", ("gy", "gz")),
        P("gx", ("gy", "gz")),
        P("gx", ("gy", "gz")),
        P(("gy", "gz"), "gx"),
    )
    out_specs = (P("gy", "gx"), P("gx", ("gy", "gz")), P("gx", ("gy", "gz")), P(("gy", "gz"), "gx"))
    return jax.shard_map(shards, mesh=mesh, in_specs=in_specs, out_specs=out_specs, check_vma=False)
```

time: 952 us -> 669 us (0.70)
  waiting for transfers between devices: 749 us -> 202 us
  starting transfers between devices: 0.67 us -> 147 us
  other arithmetic: 14.3 us -> 66.6 us
  matrix products: 133 us -> 175 us
  local copies, waits for them, and re-layouts: 40.1 us -> 50.7 us
    psum x1 -> x0, waiting for transfers between devices: 461 us -> none  [shards(): grad_hidden = lax.psum(local_sum, 'gx')]
    all_gather x4 -> x1, waiting for transfers between devices: 226 us -> 0.02 us  [shards(): activations_all = lax.all_gather(activations, 'gy', axis=0, tiled=True)]
    ppermute x0 -> x75, waiting for transfers between devices: none -> 178 us  [the longest x27 122 us: line_gather(): lax.ppermute(from_right, axis, [(i, i - 1) for i in range(1, n - s + 1)])]
    ppermute x0 -> x75, starting transfers between devices: none -> 147 us  [the longest x27 53.2 us: line_gather(): lax.ppermute(from_left, axis, [(i, i + 1) for i in range(s - 1, n - 1)])]
    convert_element_type x1 -> x36, other arithmetic: 2.08 us -> 62.9 us  [the longest x11 23.9 us: swiglu_grads(): hidden = (gate_val * sigmoid * up_val).astype(BF)]
    dot_general x6 -> x18, matrix products: 133 us -> 175 us  [the longest x3 43.1 us: shards(): lax.dot_general(grad_up, lax.slice_in_dim(up_weight, at, at + size, axis=...]
    unnamed x5 -> x248, local copies, waits for them, and re-layouts: 40.1 us -> 2.09 us
    reduce_scatter x1 -> x0, waiting for transfers between devices: 22 us -> none  [shards(): lax.psum_scatter(terms(jnp.int32(0), lax.axis_size(('gy', 'gz')) * share_...]
  transfers between devices with their start and end apart: 7 -> 77, of which waited for: 5 -> 25; matrix products, arithmetic and copies ran while one was open for 19% -> 37% of each run, Pallas kernels for 0% -> 0%
where the time goes in v1:
time: 669 us; the launch traced here: 659 us
  waiting for transfers between devices  202 us (30%)
  matrix products  175 us (26%)
  starting transfers between devices  147 us (22%)
  other arithmetic  66.6 us (10%)
  local copies, waits for them, and re-layouts  50.7 us (8%)
  between operations  18.3 us (3%)
    ppermute x27, waiting for transfers between devices, line_gather(): lax.ppermute(from_right, axis, [(i, i - 1) for i in range(1, n - s + 1)])  122 us
    ppermute x27, starting transfers between devices, line_gather(): lax.ppermute(from_left, axis, [(i, i + 1) for i in range(s - 1, n - 1)])  53.2 us
    ppermute x9, starting transfers between devices, line_scatter(): lax.ppermute(to_right.astype(BF), axis, [(i, i + 1) for i in range(min(t,...  45 us
    dot_general x3, matrix products, shards(): lax.dot_general(grad_up, lax.slice_in_dim(up_weight, at, at + size, axis=...  43.1 us
    ppermute x27, starting transfers between devices, line_gather(): lax.ppermute(from_right, axis, [(i, i - 1) for i in range(1, n - s + 1)])  35.3 us
    dot_general x3, matrix products, shards(): lax.dot_general(grad_gate, lax.slice_in_dim(gate_weight, at, at + size, a...  32.4 us
    dot_general x3, matrix products, shards(): lax.dot_general(act, grad_up, over_rows, preferred_element_type=F32)  26.9 us
    dot_general x3, matrix products, shards(): lax.dot_general(cot, lax.slice_in_dim(down_weight, at, at + size, axis=0)...  25.5 us
  transfers between devices with their start and end apart: 77, of which 25 were waited for; matrix products, arithmetic and copies ran while one was open for 37% of the time, Pallas kernels for 0%

profile of v1, /device:TPU:0, one launch (start us, length us, event | category | flops | bytes accessed | tf_op | source)
XLA Modules:
  0.0 659.0 jit_solution(11141083498765120991)
XLA Ops:
  24.0 22.7 %all-gather.3.cloned.1.call-done = bf16[1024,2048]{1,0:T(8,128)(2,1)} async-done(((bf16[256,2048]{1,0:T(8,128)(2,1)}), bf16[1024,2048]{1,0:T(8,128)(2,1)}) %all-gather.3.cloned.1.call-update) | async-done | bytes 4194320 | tf_op jit(solution)/shard_map/all_gather | solution.py:95
  49.3 9.6 %fusion.13 = f32[1024,1280]{1,0:T(8,128)S(1)} fusion(bf16[3328,2048]{1,0:T(8,128)(2,1)} %param.13, bf16[256,2048]{1,0:T(8,128)(2,1)S(1)} %get-tuple-element.51, bf16[256,2048]{1,0:T(8,128)(2,1)S(1)} %get-tuple-element.52, bf16[256,2048]{1,0:T(8,128)(2,1)S(1)} %get-tuple-element.53, bf16[256,2048]{1,0:T(8,128)(2,1)S(1)} %get-tuple-element.50), kind=kOutput, calls=%fused_computation.21 | convolution fusion | flops 5385486336 | bytes 14680064 | tf_op jit(solution)/shard_map/dot_general | solution.py:116
  67.4 9.4 %collective-permute-done = bf16[256,1280]{1,0:T(8,128)(2,1)S(1)} collective-permute-done((bf16[256,1280]{1,0:T(8,128)(2,1)S(1)}, bf16[256,1280]{1,0:T(8,128)(2,1)S(1)}, u32[]{:S(2)}, u32[]{:S(2)}) %collective-permute-start) | collective-permute-done | bytes 655392 | tf_op jit(solution)/shard_map/ppermute | solution.py:46
  87.2 12.4 %collective-permute-done.16 = bf16[256,1280]{1,0:T(8,128)(2,1)} collective-permute-done((bf16[256,1280]{1,0:T(8,128)(2,1)}, bf16[256,1280]{1,0:T(8,128)(2,1)}, u32[]{:S(2)}, u32[]{:S(2)}) %collective-permute-start.16) | collective-permute-done | bytes 655392 | tf_op jit(solution)/shard_map/ppermute | solution.py:34
  111.0 8.1 %collective-permute-done.13 = bf16[256,1280]{1,0:T(8,128)(2,1)S(1)} collective-permute-done((bf16[256,1280]{1,0:T(8,128)(2,1)S(1)}, bf16[256,1280]{1,0:T(8,128)(2,1)S(1)}, u32[]{:S(2)}, u32[]{:S(2)}) %collective-permute-start.13) | collective-permute-done | bytes 655392 | tf_op jit(solution)/shard_map/ppermute | solution.py:34
  119.2 12.1 %collective-permute-done.17 = bf16[256,1280]{1,0:T(8,128)(2,1)S(1)} collective-permute-done((bf16[256,1280]{1,0:T(8,128)(2,1)}, bf16[256,1280]{1,0:T(8,128)(2,1)S(1)}, u32[]{:S(2)}, u32[]{:S(2)}) %collective-permute-start.17) | collective-permute-done | bytes 655392 | tf_op jit(solution)/shard_map/ppermute | solution.py:34
  139.5 10.5 %fusion.7 = f32[1024,1280]{1,0:T(8,128)} fusion(bf16[3328,2048]{1,0:T(8,128)(2,1)} %param.13, bf16[256,2048]{1,0:T(8,128)(2,1)S(1)} %copy-done.64, bf16[256,2048]{1,0:T(8,128)(2,1)S(1)} %copy-done.69, bf16[256,2048]{1,0:T(8,128)(2,1)S(1)} %copy-done.74, bf16[256,2048]{1,0:T(8,128)(2,1)S(1)} %copy-done.59), kind=kOutput, calls=%fused_computation.15 | convolution fusion | flops 5385486336 | bytes 14680064 | tf_op jit(solution)/shard_map/dot_general | solution.py:116
  235.6 8.4 %convolution_convert_fusion.1 = bf16[1280,2048]{1,0:T(8,128)(2,1)S(1)} fusion(bf16[256,1280]{1,0:T(8,128)(2,1)S(1)} %copy-done.104, bf16[256,1280]{1,0:T(8,128)(2,1)S(1)} %copy-done.103, bf16[256,1280]{1,0:T(8,128)(2,1)} %get-tuple-element.22, bf16[256,1280]{1,0:T(8,128)(2,1)} %get-tuple-element.54, bf16[256,2048]{1,0:T(8,128)(2,1)} %copy-done.63, ...), kind=kOutput, calls=%fused_computation.4 | convolution fusion | flops 5398593536 | bytes 12058624 | tf_op jit(solution)/shard_map/dot_general | solution.py:149
  244.1 8.4 %dynamic_update_slice.33 = bf16[3328,2048]{1,0:T(8,128)(2,1)} pad(bf16[1280,2048]{1,0:T(8,128)(2,1)S(1)} %convolution_convert_fusion.1, bf16[]{:T(256)} %constant.119.clone.1), padding=0_2048x0_0 | pad | bytes 18874370 | tf_op jit(solution)/shard_map/dynamic_update_slice | solution.py:152
  266.2 7.7 %collective-permute-done.65 = bf16[256,768]{1,0:T(8,128)(2,1)S(1)} collective-permute-done((bf16[256,768]{1,0:T(8,128)(2,1)S(1)}, bf16[256,768]{1,0:T(8,128)(2,1)S(1)}, u32[]{:S(2)}, u32[]{:S(2)}) %collective-permute-start.65) | collective-permute-done | bytes 393248 | tf_op jit(solution)/shard_map/ppermute | solution.py:34
  291.3 10.8 %collective-permute-done.8 = bf16[256,1280]{1,0:T(8,128)(2,1)} collective-permute-done((bf16[256,1280]{1,0:T(8,128)(2,1)}, bf16[256,1280]{1,0:T(8,128)(2,1)}, u32[]{:S(2)}, u32[]{:S(2)}) %collective-permute-start.8) | collective-permute-done | bytes 655392 | tf_op jit(solution)/shard_map/ppermute | solution.py:34
  306.6 9.5 %collective-permute-done.36 = bf16[256,1280]{1,0:T(8,128)(2,1)S(1)} collective-permute-done((bf16[256,1280]{1,0:T(8,128)(2,1)}, bf16[256,1280]{1,0:T(8,128)(2,1)S(1)}, u32[]{:S(2)}, u32[]{:S(2)}) %collective-permute-start.36) | collective-permute-done | bytes 655392 | tf_op jit(solution)/shard_map/ppermute | solution.py:34
  316.8 7.3 %collective-permute-done.40 = bf16[256,1280]{1,0:T(8,128)(2,1)S(1)} collective-permute-done((bf16[256,1280]{1,0:T(8,128)(2,1)S(1)}, bf16[256,1280]{1,0:T(8,128)(2,1)S(1)}, u32[]{:S(2)}, u32[]{:S(2)}) %collective-permute-start.40) | collective-permute-done | bytes 655392 | tf_op jit(solution)/shard_map/ppermute | solution.py:34
  336.5 11.6 %collective-permute-done.37 = bf16[256,1280]{1,0:T(8,128)(2,1)S(1)} collective-permute-done((bf16[256,1280]{1,0:T(8,128)(2,1)S(1)}, bf16[256,1280]{1,0:T(8,128)(2,1)S(1)}, u32[]{:S(2)}, u32[]{:S(2)}) %collective-permute-start.37) | collective-permute-done | bytes 655392 | tf_op jit(solution)/shard_map/ppermute | solution.py:34
  350.3 11.7 %collective-permute-done.41 = bf16[256,1280]{1,0:T(8,128)(2,1)S(1)} collective-permute-done((bf16[256,1280]{1,0:T(8,128)(2,1)S(1)}, bf16[256,1280]{1,0:T(8,128)(2,1)S(1)}, u32[]{:S(2)}, u32[]{:S(2)}) %collective-permute-start.41) | collective-permute-done | bytes 655392 | tf_op jit(solution)/shard_map/ppermute | solution.py:34
  363.6 9.3 %fusion = bf16[3328,2048]{1,0:T(8,128)(2,1)} fusion(bf16[3328,2048]{1,0:T(8,128)(2,1)} %dynamic_update_slice.33, bf16[256,1280]{1,0:T(8,128)(2,1)S(1)} %get-tuple-element.20, bf16[256,1280]{1,0:T(8,128)(2,1)S(1)} %get-tuple-element.18, bf16[256,1280]{1,0:T(8,128)(2,1)S(1)} %get-tuple-element.16, bf16[256,1280]{1,0:T(8,128)(2,1)} %get-tuple-element.56, ...), kind=kOutput, calls=%fused_computation.3 | convolution fusion | flops 5398593536 | bytes 12058624 | tf_op jit(solution)/shard_map/dot_general | solution.py:149
  396.8 10.5 %fusion.11 = f32[1024,2048]{1,0:T(8,128)} fusion(bf16[2048,3328]{1,0:T(8,128)(2,1)} %param.11, bf16[256,1280]{1,0:T(8,128)(2,1)} %get-tuple-element.68, bf16[256,1280]{1,0:T(8,128)(2,1)} %get-tuple-element.66, bf16[256,1280]{1,0:T(8,128)(2,1)} %get-tuple-element.64, bf16[256,1280]{1,0:T(8,128)(2,1)} %get-tuple-element.55), kind=kOutput, calls=%fused_computation.19 | convolution fusion | flops 5379194880 | bytes 16252928 | tf_op jit(solution)/shard_map/dot_general | solution.py:141
  408.7 12.1 %fusion.9 = f32[1024,2048]{1,0:T(8,128)} fusion(bf16[2048,3328]{1,0:T(8,128)(2,1)} %param.12, bf16[256,1280]{1,0:T(8,128)(2,1)S(1)} %copy-done.89, bf16[256,1280]{1,0:T(8,128)(2,1)S(1)} %copy-done.87, bf16[256,1280]{1,0:T(8,128)(2,1)S(1)} %copy-done.90, bf16[256,1280]{1,0:T(8,128)(2,1)S(1)} %copy-done.86), kind=kOutput, calls=%fused_computation.17 | convolution fusion | flops 5379194880 | bytes 16252928 | tf_op jit(solution)/shard_map/dot_general | solution.py:144
  428.8 8.2 %convolution_convert_fusion.5 = bf16[2048,1280]{1,0:T(8,128)(2,1)} fusion(bf16[256,1280]{1,0:T(8,128)(2,1)S(1)} %copy-done.100, bf16[256,1280]{1,0:T(8,128)(2,1)S(1)} %copy-done.92, bf16[256,1280]{1,0:T(8,128)(2,1)S(1)} %copy-done.101, bf16[256,1280]{1,0:T(8,128)(2,1)S(1)} %copy-done.105, bf16[256,2048]{1,0:T(8,128)(2,1)S(1)} %copy-done.80, ...), kind=kOutput, calls=%fused_computation.10 | convolution fusion | flops 5398593536 | bytes 12058624 | tf_op jit(solution)/shard_map/dot_general | solution.py:150
  440.8 10.2 %collective-permute-start.50 = (bf16[256,768]{1,0:T(8,128)(2,1)S(1)}, bf16[256,768]{1,0:T(8,128)(2,1)S(1)}, u32[]{:S(2)}, u32[]{:S(2)}) collective-permute-start(bf16[256,768]{1,0:T(8,128)(2,1)S(1)} %get-tuple-element.59), channel_id=1, source_target_pairs={{0,8},{8,16},{16,24},{1,9},{9,17},{17,25},{2,10},{10,18},{18,26},{... | collective-permute-start | bytes 1179656 | tf_op jit(solution)/shard_map/ppermute | solution.py:46
  461.5 7.1 %collective-permute-done.53 = bf16[256,768]{1,0:T(8,128)(2,1)S(1)} collective-permute-done((bf16[256,768]{1,0:T(8,128)(2,1)S(1)}, bf16[256,768]{1,0:T(8,128)(2,1)S(1)}, u32[]{:S(2)}, u32[]{:S(2)}) %collective-permute-start.53) | collective-permute-done | bytes 393248 | tf_op jit(solution)/shard_map/ppermute | solution.py:49
  480.3 12.4 %fusion.5 = f32[1024,2048]{1,0:T(8,128)} fusion(bf16[2048,3328]{1,0:T(8,128)(2,1)} %param.11, bf16[256,1280]{1,0:T(8,128)(2,1)S(1)} %get-tuple-element.74, bf16[256,1280]{1,0:T(8,128)(2,1)S(1)} %get-tuple-element.72, bf16[256,1280]{1,0:T(8,128)(2,1)S(1)} %get-tuple-element.70, bf16[256,1280]{1,0:T(8,128)(2,1)S(1)} %fusion.64), kind=kOutput, calls=%fused_computation.13 | convolution fusion | flops 5379194880 | bytes 16252928 | tf_op jit(solution)/shard_map/dot_general | solution.py:141
  494.8 12.1 %fusion.3 = f32[1024,2048]{1,0:T(8,128)} fusion(bf16[2048,3328]{1,0:T(8,128)(2,1)} %param.12, bf16[256,1280]{1,0:T(8,128)(2,1)S(1)} %get-tuple-element.73, bf16[256,1280]{1,0:T(8,128)(2,1)S(1)} %get-tuple-element.71, bf16[256,1280]{1,0:T(8,128)(2,1)S(1)} %get-tuple-element.69, bf16[256,1280]{1,0:T(8,128)(2,1)S(1)} %copy-done.88), kind=kOutput, calls=%fused_computation.11 | convolution fusion | flops 5379194880 | bytes 16252928 | tf_op jit(solution)/shard_map/dot_general | solution.py:144
  506.9 7.3 %collective-permute-done.56 = bf16[256,768]{1,0:T(8,128)(2,1)S(1)} collective-permute-done((bf16[256,768]{1,0:T(8,128)(2,1)S(1)}, bf16[256,768]{1,0:T(8,128)(2,1)S(1)}, u32[]{:S(2)}, u32[]{:S(2)}) %collective-permute-start.56) | collective-permute-done | bytes 393248 | tf_op jit(solution)/shard_map/ppermute | solution.py:34
  517.9 6.9 %collective-permute-done.57 = bf16[256,768]{1,0:T(8,128)(2,1)S(1)} collective-permute-done((bf16[256,768]{1,0:T(8,128)(2,1)S(1)}, bf16[256,768]{1,0:T(8,128)(2,1)S(1)}, u32[]{:S(2)}, u32[]{:S(2)}) %collective-permute-start.57) | collective-permute-done | bytes 393248 | tf_op jit(solution)/shard_map/ppermute | solution.py:34
  525.4 9.4 %fusion.19 = f32[1024,2048]{1,0:T(8,128)} fusion(bf16[2048,3328]{1,0:T(8,128)(2,1)} %param.11, bf16[256,768]{1,0:T(8,128)(2,1)S(1)} %get-tuple-element.80, bf16[256,768]{1,0:T(8,128)(2,1)S(1)} %get-tuple-element.78, bf16[256,768]{1,0:T(8,128)(2,1)S(1)} %get-tuple-element.76, bf16[256,768]{1,0:T(8,128)(2,1)S(1)} %fusion.134), kind=kOutput, calls=%fused_computation.34 | convolution fusion | flops 3227516928 | bytes 13107200 | tf_op jit(solution)/shard_map/dot_general | solution.py:141
  534.9 18.9 %add_add_fusion = f32[1024,2048]{1,0:T(8,128)} fusion(f32[1024,2048]{1,0:T(8,128)} %fusion.19, f32[1024,2048]{1,0:T(8,128)} %fusion.5, f32[1024,2048]{1,0:T(8,128)} %fusion.3, f32[1024,2048]{1,0:T(8,128)} %fusion.11, f32[1024,2048]{1,0:T(8,128)} %fusion.9, bf16[2048,3328]{1,0:T(8,128)(2,1)} %param.12, bf16[256,768]{1,0:T(8,128)(2,1)S(1)} %get-tuple-element.79, ...), kind=kOutput, calls=%fused_computation.1 | convolution fusion | flops 3238002688 | bytes 55050240 | tf_op jit(solution)/shard_map/dot_general | solution.py:144
  559.1 11.2 %convolution_convert_fusion.3 = bf16[2048,1280]{1,0:T(8,128)(2,1)} fusion(bf16[256,1280]{1,0:T(8,128)(2,1)} %get-tuple-element.67, bf16[256,1280]{1,0:T(8,128)(2,1)} %get-tuple-element.65, bf16[256,1280]{1,0:T(8,128)(2,1)} %get-tuple-element.63, bf16[256,1280]{1,0:T(8,128)(2,1)} %get-tuple-element.30, bf16[256,2048]{1,0:T(8,128)(2,1)} %get-tuple-element.47, ...), kind=kOutput, calls=%fused_computation.7 | convolution fusion | flops 5398593536 | bytes 12058624 | tf_op jit(solution)/shard_map/dot_general | solution.py:151
  588.5 10.7 %fusion.2 = bf16[2048,3328]{1,0:T(8,128)(2,1)} fusion(bf16[2048,3328]{1,0:T(8,128)(2,1)} %dynamic_update_slice.27, bf16[256,1280]{1,0:T(8,128)(2,1)} %copy-done.98, bf16[256,1280]{1,0:T(8,128)(2,1)} %copy-done.95, bf16[256,1280]{1,0:T(8,128)(2,1)} %copy-done.99, bf16[256,1280]{1,0:T(8,128)(2,1)} %copy-done.91, bf16[256,2048]{1,0:T(8,128)(2,1)} %get-tuple-element.47, ...), kind=kOutput, calls=%fused_computation.9 | convolution fusion | flops 5398593536 | bytes 12058624 | tf_op jit(solution)/shard_map/dot_general | solution.py:150
  600.9 10.4 %fusion.1 = bf16[2048,3328]{1,0:T(8,128)(2,1)} fusion(bf16[2048,3328]{1,0:T(8,128)(2,1)} %dynamic_update_slice.30, bf16[256,1280]{1,0:T(8,128)(2,1)} %copy-done.96, bf16[256,1280]{1,0:T(8,128)(2,1)} %copy-done.93, bf16[256,1280]{1,0:T(8,128)(2,1)} %copy-done.97, bf16[256,1280]{1,0:T(8,128)(2,1)} %get-tuple-element.32, bf16[256,2048]{1,0:T(8,128)(2,1)S(1)} %copy-done.81, ...), kind=kOutput, calls=%fused_computation.6 | convolution fusion | flops 5398593536 | bytes 12058624 | tf_op jit(solution)/shard_map/dot_general | solution.py:151
  611.3 14.3 %collective-permute-done.73 = bf16[1,256,2048]{2,1,0:T(8,128)(2,1)S(1)} collective-permute-done((bf16[1,256,2048]{2,1,0:T(8,128)(2,1)S(1)}, bf16[1,256,2048]{2,1,0:T(8,128)(2,1)S(1)}, u32[]{:S(2)}, u32[]{:S(2)}) %collective-permute-start.73) | collective-permute-done | bytes 1048608 | tf_op jit(solution)/shard_map/ppermute | solution.py:68
  638.1 12.4 %collective-permute-done.74 = bf16[256,2048]{1,0:T(8,128)(2,1)S(1)} collective-permute-done((bf16[256,2048]{1,0:T(8,128)(2,1)S(1)}, bf16[256,2048]{1,0:T(8,128)(2,1)S(1)}, u32[]{:S(2)}, u32[]{:S(2)}) %collective-permute-start.74) | collective-permute-done | bytes 1048608 | tf_op jit(solution)/shard_map/ppermute | solution.py:161
  (449 shorter events, 297.0 us)
Async XLA Ops:
  7.2 39.6 %all-gather.3.cloned.1.call-start = ((), (), s32[]{:S(2)}) async-start(), calls=%async_computation | async-start | bytes 5242880 | tf_op jit(solution)/shard_map/all_gather | solution.py:95
  7.9 192.8 %all-gather.5.cloned.1.call-start = ((), (), s32[]{:S(2)}) async-start(), calls=%async_computation.1 | async-start | bytes 5242880 | tf_op jit(solution)/shard_map/all_gather | solution.py:96
  9.1 53.4 %collective-permute-start.10 = (bf16[256,1280]{1,0:T(8,128)(2,1)S(1)}, bf16[256,1280]{1,0:T(8,128)(2,1)S(1)}, u32[]{:S(2)}, u32[]{:S(2)}) collective-permute-start(bf16[256,1280]{1,0:T(8,128)(2,1)S(1)} %slice.125), channel_id=1, source_target_pairs={{0,8},{8,16},{16,24},{1,9},{9,17},{17,25},{2,10},{10,18},{18,26},{... | collective-permute-start | bytes 1966088 | tf_op jit(solution)/shard_map/ppermute | solution.py:33
  14.1 50.7 %collective-permute-start.11 = (bf16[256,1280]{1,0:T(8,128)(2,1)S(1)}, bf16[256,1280]{1,0:T(8,128)(2,1)S(1)}, u32[]{:S(2)}, u32[]{:S(2)}) collective-permute-start(bf16[256,1280]{1,0:T(8,128)(2,1)S(1)} %slice.125), channel_id=1, source_target_pairs={{8,0},{16,8},{24,16},{9,1},{17,9},{25,17},{10,2},{18,10},{26,18},{... | collective-permute-start | bytes 1966088 | tf_op jit(solution)/shard_map/ppermute | solution.py:34
  17.3 45.9 %collective-permute-start.14 = (bf16[256,1280]{1,0:T(8,128)(2,1)}, bf16[256,1280]{1,0:T(8,128)(2,1)}, u32[]{:S(2)}, u32[]{:S(2)}) collective-permute-start(bf16[256,1280]{1,0:T(8,128)(2,1)} %slice.126), channel_id=1, source_target_pairs={{0,8},{8,16},{16,24},{1,9},{9,17},{17,25},{2,10},{10,18},{18,26},{... | collective-permute-start | bytes 1966088 | tf_op jit(solution)/shard_map/ppermute | solution.py:33
  22.7 43.4 %collective-permute-start.15 = (bf16[256,1280]{1,0:T(8,128)(2,1)}, bf16[256,1280]{1,0:T(8,128)(2,1)}, u32[]{:S(2)}, u32[]{:S(2)}) collective-permute-start(bf16[256,1280]{1,0:T(8,128)(2,1)} %slice.126), channel_id=1, source_target_pairs={{8,0},{16,8},{24,16},{9,1},{17,9},{25,17},{10,2},{18,10},{26,18},{... | collective-permute-start | bytes 1966088 | tf_op jit(solution)/shard_map/ppermute | solution.py:34
  66.1 33.5 %collective-permute-start.16 = (bf16[256,1280]{1,0:T(8,128)(2,1)}, bf16[256,1280]{1,0:T(8,128)(2,1)}, u32[]{:S(2)}, u32[]{:S(2)}) collective-permute-start(bf16[256,1280]{1,0:T(8,128)(2,1)} %collective-permute-done.15), channel_id=1, source_target_pairs={{8,0},{16,8},{9,1},{17,9},{10,2},{18,10},{11,3},{19,11},{12,4},{20... | collective-permute-start | bytes 1966088 | tf_op jit(solution)/shard_map/ppermute | solution.py:34
  76.9 26.8 %collective-permute-start.3 = (bf16[256,1280]{1,0:T(8,128)(2,1)S(1)}, bf16[256,1280]{1,0:T(8,128)(2,1)}, u32[]{:S(2)}, u32[]{:S(2)}) collective-permute-start(bf16[256,1280]{1,0:T(8,128)(2,1)S(1)} %get-tuple-element.45), channel_id=1, source_target_pairs={{24,16},{25,17},{26,18},{27,19},{28,20},{29,21},{30,22},{31,23}} | collective-permute-start | bytes 1966088 | tf_op jit(solution)/shard_map/ppermute | solution.py:49
  79.4 25.6 %collective-permute-start.1 = (bf16[256,1280]{1,0:T(8,128)(2,1)}, bf16[256,1280]{1,0:T(8,128)(2,1)}, u32[]{:S(2)}, u32[]{:S(2)}) collective-permute-start(bf16[256,1280]{1,0:T(8,128)(2,1)} %add_convert_fusion.7), channel_id=1, source_target_pairs={{0,8},{8,16},{1,9},{9,17},{2,10},{10,18},{3,11},{11,19},{4,12},{12... | collective-permute-start | bytes 1966088 | tf_op jit(solution)/shard_map/ppermute | solution.py:46
  103.7 27.6 %collective-permute-start.17 = (bf16[256,1280]{1,0:T(8,128)(2,1)}, bf16[256,1280]{1,0:T(8,128)(2,1)S(1)}, u32[]{:S(2)}, u32[]{:S(2)}) collective-permute-start(bf16[256,1280]{1,0:T(8,128)(2,1)} %collective-permute-done.16), channel_id=1, source_target_pairs={{8,0},{9,1},{10,2},{11,3},{12,4},{13,5},{14,6},{15,7}} | collective-permute-start | bytes 1966088 | tf_op jit(solution)/shard_map/ppermute | solution.py:34
  107.3 28.3 %collective-permute-start.4 = (bf16[256,1280]{1,0:T(8,128)(2,1)S(1)}, bf16[256,1280]{1,0:T(8,128)(2,1)S(1)}, u32[]{:S(2)}, u32[]{:S(2)}) collective-permute-start(bf16[256,1280]{1,0:T(8,128)(2,1)S(1)} %get-tuple-element.43), channel_id=1, source_target_pairs={{16,8},{24,16},{17,9},{25,17},{18,10},{26,18},{19,11},{27,19},{20,... | collective-permute-start | bytes 1966088 | tf_op jit(solution)/shard_map/ppermute | solution.py:49
  133.0 25.4 %collective-permute-start.2 = (bf16[256,1280]{1,0:T(8,128)(2,1)S(1)}, bf16[256,1280]{1,0:T(8,128)(2,1)S(1)}, u32[]{:S(2)}, u32[]{:S(2)}) collective-permute-start(bf16[256,1280]{1,0:T(8,128)(2,1)S(1)} %get-tuple-element.42), channel_id=1, source_target_pairs={{0,8},{8,16},{16,24},{1,9},{9,17},{17,25},{2,10},{10,18},{18,26},{... | collective-permute-start | bytes 1966088 | tf_op jit(solution)/shard_map/ppermute | solution.py:46
  171.0 28.4 %collective-permute-start.59 = (bf16[256,768]{1,0:T(8,128)(2,1)S(1)}, bf16[256,768]{1,0:T(8,128)(2,1)}, u32[]{:S(2)}, u32[]{:S(2)}) collective-permute-start(bf16[256,768]{1,0:T(8,128)(2,1)S(1)} %get-tuple-element.5), channel_id=1, source_target_pairs={{8,0},{16,8},{24,16},{9,1},{17,9},{25,17},{10,2},{18,10},{26,18},{... | collective-permute-start | bytes 1179656 | tf_op jit(solution)/shard_map/ppermute | solution.py:34
  172.3 32.9 %collective-permute-start.62 = (bf16[256,768]{1,0:T(8,128)(2,1)S(1)}, bf16[256,768]{1,0:T(8,128)(2,1)}, u32[]{:S(2)}, u32[]{:S(2)}) collective-permute-start(bf16[256,768]{1,0:T(8,128)(2,1)S(1)} %get-tuple-element.6), channel_id=1, source_target_pairs={{0,8},{8,16},{16,24},{1,9},{9,17},{17,25},{2,10},{10,18},{18,26},{... | collective-permute-start | bytes 1179656 | tf_op jit(solution)/shard_map/ppermute | solution.py:33
  177.6 28.4 %collective-permute-start.63 = (bf16[256,768]{1,0:T(8,128)(2,1)S(1)}, bf16[256,768]{1,0:T(8,128)(2,1)}, u32[]{:S(2)}, u32[]{:S(2)}) collective-permute-start(bf16[256,768]{1,0:T(8,128)(2,1)S(1)} %get-tuple-element.6), channel_id=1, source_target_pairs={{8,0},{16,8},{24,16},{9,1},{17,9},{25,17},{10,2},{18,10},{26,18},{... | collective-permute-start | bytes 1179656 | tf_op jit(solution)/shard_map/ppermute | solution.py:34
  219.3 39.7 %collective-permute-start.6 = (bf16[256,1280]{1,0:T(8,128)(2,1)S(1)}, bf16[256,1280]{1,0:T(8,128)(2,1)}, u32[]{:S(2)}, u32[]{:S(2)}) collective-permute-start(bf16[256,1280]{1,0:T(8,128)(2,1)S(1)} %copy-done.5), channel_id=1, source_target_pairs={{0,8},{8,16},{16,24},{1,9},{9,17},{17,25},{2,10},{10,18},{18,26},{... | collective-permute-start | bytes 1966088 | tf_op jit(solution)/shard_map/ppermute | solution.py:33
  225.2 38.4 %collective-permute-start.7 = (bf16[256,1280]{1,0:T(8,128)(2,1)S(1)}, bf16[256,1280]{1,0:T(8,128)(2,1)}, u32[]{:S(2)}, u32[]{:S(2)}) collective-permute-start(bf16[256,1280]{1,0:T(8,128)(2,1)S(1)} %copy-done.5), channel_id=1, source_target_pairs={{8,0},{16,8},{24,16},{9,1},{17,9},{25,17},{10,2},{18,10},{26,18},{... | collective-permute-start | bytes 1966088 | tf_op jit(solution)/shard_map/ppermute | solution.py:34
  226.5 49.0 %collective-permute-start.27 = (bf16[256,1280]{1,0:T(8,128)(2,1)}, bf16[256,1280]{1,0:T(8,128)(2,1)}, u32[]{:S(2)}, u32[]{:S(2)}) collective-permute-start(bf16[256,1280]{1,0:T(8,128)(2,1)} %get-tuple-element.41), channel_id=1, source_target_pairs={{24,16},{25,17},{26,18},{27,19},{28,20},{29,21},{30,22},{31,23}} | collective-permute-start | bytes 1966088 | tf_op jit(solution)/shard_map/ppermute | solution.py:49
  275.5 26.6 %collective-permute-start.8 = (bf16[256,1280]{1,0:T(8,128)(2,1)}, bf16[256,1280]{1,0:T(8,128)(2,1)}, u32[]{:S(2)}, u32[]{:S(2)}) collective-permute-start(bf16[256,1280]{1,0:T(8,128)(2,1)} %collective-permute-done.7), channel_id=1, source_target_pairs={{8,0},{16,8},{9,1},{17,9},{10,2},{18,10},{11,3},{19,11},{12,4},{20... | collective-permute-start | bytes 1966088 | tf_op jit(solution)/shard_map/ppermute | solution.py:34
  279.5 47.3 %collective-permute-start.25 = (bf16[256,1280]{1,0:T(8,128)(2,1)S(1)}, bf16[256,1280]{1,0:T(8,128)(2,1)S(1)}, u32[]{:S(2)}, u32[]{:S(2)}) collective-permute-start(bf16[256,1280]{1,0:T(8,128)(2,1)S(1)} %copy-done.94), channel_id=1, source_target_pairs={{0,8},{8,16},{1,9},{9,17},{2,10},{10,18},{3,11},{11,19},{4,12},{12... | collective-permute-start | bytes 1966088 | tf_op jit(solution)/shard_map/ppermute | solution.py:46
  288.7 27.4 %collective-permute-start.36 = (bf16[256,1280]{1,0:T(8,128)(2,1)}, bf16[256,1280]{1,0:T(8,128)(2,1)S(1)}, u32[]{:S(2)}, u32[]{:S(2)}) collective-permute-start(bf16[256,1280]{1,0:T(8,128)(2,1)} %collective-permute-done.35), channel_id=1, source_target_pairs={{8,0},{16,8},{9,1},{17,9},{10,2},{18,10},{11,3},{19,11},{12,4},{20... | collective-permute-start | bytes 1966088 | tf_op jit(solution)/shard_map/ppermute | solution.py:34
  290.0 34.1 %collective-permute-start.40 = (bf16[256,1280]{1,0:T(8,128)(2,1)S(1)}, bf16[256,1280]{1,0:T(8,128)(2,1)S(1)}, u32[]{:S(2)}, u32[]{:S(2)}) collective-permute-start(bf16[256,1280]{1,0:T(8,128)(2,1)S(1)} %collective-permute-done.39), channel_id=1, source_target_pairs={{8,0},{16,8},{9,1},{17,9},{10,2},{18,10},{11,3},{19,11},{12,4},{20... | collective-permute-start | bytes 1966088 | tf_op jit(solution)/shard_map/ppermute | solution.py:34
  302.2 25.9 %collective-permute-start.28 = (bf16[256,1280]{1,0:T(8,128)(2,1)S(1)}, bf16[256,1280]{1,0:T(8,128)(2,1)S(1)}, u32[]{:S(2)}, u32[]{:S(2)}) collective-permute-start(bf16[256,1280]{1,0:T(8,128)(2,1)S(1)} %add_convert_fusion.1), channel_id=1, source_target_pairs={{16,8},{24,16},{17,9},{25,17},{18,10},{26,18},{19,11},{27,19},{20,... | collective-permute-start | bytes 1966088 | tf_op jit(solution)/shard_map/ppermute | solution.py:49
  326.8 35.3 %collective-permute-start.41 = (bf16[256,1280]{1,0:T(8,128)(2,1)S(1)}, bf16[256,1280]{1,0:T(8,128)(2,1)S(1)}, u32[]{:S(2)}, u32[]{:S(2)}) collective-permute-start(bf16[256,1280]{1,0:T(8,128)(2,1)S(1)} %collective-permute-done.40), channel_id=1, source_target_pairs={{8,0},{9,1},{10,2},{11,3},{12,4},{13,5},{14,6},{15,7}} | collective-permute-start | bytes 1966088 | tf_op jit(solution)/shard_map/ppermute | solution.py:34
  328.1 44.8 %collective-permute-start.21 = (bf16[256,1280]{1,0:T(8,128)(2,1)}, bf16[256,1280]{1,0:T(8,128)(2,1)}, u32[]{:S(2)}, u32[]{:S(2)}) collective-permute-start(bf16[256,1280]{1,0:T(8,128)(2,1)} %collective-permute-done.18), channel_id=1, source_target_pairs={{16,24},{17,25},{18,26},{19,27},{20,28},{21,29},{22,30},{23,31}} | collective-permute-start | bytes 1966088 | tf_op jit(solution)/shard_map/ppermute | solution.py:33
  331.0 45.2 %collective-permute-start.9 = (bf16[256,1280]{1,0:T(8,128)(2,1)}, bf16[256,1280]{1,0:T(8,128)(2,1)}, u32[]{:S(2)}, u32[]{:S(2)}) collective-permute-start(bf16[256,1280]{1,0:T(8,128)(2,1)} %collective-permute-done.8), channel_id=1, source_target_pairs={{8,0},{9,1},{10,2},{11,3},{12,4},{13,5},{14,6},{15,7}} | collective-permute-start | bytes 1966088 | tf_op jit(solution)/shard_map/ppermute | solution.py:34
  332.4 51.4 %collective-permute-start.29 = (bf16[256,1280]{1,0:T(8,128)(2,1)}, bf16[256,1280]{1,0:T(8,128)(2,1)}, u32[]{:S(2)}, u32[]{:S(2)}) collective-permute-start(bf16[256,1280]{1,0:T(8,128)(2,1)} %get-tuple-element.39), channel_id=1, source_target_pairs={{8,0},{16,8},{24,16},{9,1},{17,9},{25,17},{10,2},{18,10},{26,18},{... | collective-permute-start | bytes 1966088 | tf_op jit(solution)/shard_map/ppermute | solution.py:49
  348.0 35.8 %collective-permute-start.26 = (bf16[256,1280]{1,0:T(8,128)(2,1)}, bf16[256,1280]{1,0:T(8,128)(2,1)}, u32[]{:S(2)}, u32[]{:S(2)}) collective-permute-start(bf16[256,1280]{1,0:T(8,128)(2,1)} %get-tuple-element.38), channel_id=1, source_target_pairs={{0,8},{8,16},{16,24},{1,9},{9,17},{17,25},{2,10},{10,18},{18,26},{... | collective-permute-start | bytes 1966088 | tf_op jit(solution)/shard_map/ppermute | solution.py:46
  439.4 29.3 %collective-permute-start.53 = (bf16[256,768]{1,0:T(8,128)(2,1)S(1)}, bf16[256,768]{1,0:T(8,128)(2,1)S(1)}, u32[]{:S(2)}, u32[]{:S(2)}) collective-permute-start(bf16[256,768]{1,0:T(8,128)(2,1)S(1)} %get-tuple-element.60), channel_id=1, source_target_pairs={{8,0},{16,8},{24,16},{9,1},{17,9},{25,17},{10,2},{18,10},{26,18},{... | collective-permute-start | bytes 1179656 | tf_op jit(solution)/shard_map/ppermute | solution.py:49
  440.8 27.8 %collective-permute-start.50 = (bf16[256,768]{1,0:T(8,128)(2,1)S(1)}, bf16[256,768]{1,0:T(8,128)(2,1)S(1)}, u32[]{:S(2)}, u32[]{:S(2)}) collective-permute-start(bf16[256,768]{1,0:T(8,128)(2,1)S(1)} %get-tuple-element.59), channel_id=1, source_target_pairs={{0,8},{8,16},{16,24},{1,9},{9,17},{17,25},{2,10},{10,18},{18,26},{... | collective-permute-start | bytes 1179656 | tf_op jit(solution)/shard_map/ppermute | solution.py:46
  559.0 40.1 %collective-permute-start.72 = (bf16[2,256,2048]{2,1,0:T(8,128)(2,1)S(1)}, bf16[2,256,2048]{2,1,0:T(8,128)(2,1)S(1)}, u32[]{:S(2)}, u32[]{:S(2)}) collective-permute-start(bf16[2,256,2048]{2,1,0:T(8,128)(2,1)S(1)} %fusion.37), channel_id=1, source_target_pairs={{0,2},{2,0},{4,6},{6,4},{1,3},{3,1},{5,7},{7,5},{8,10},{10,8},{12,... | collective-permute-start | bytes 6291464 | tf_op jit(solution)/shard_map/ppermute | solution.py:68
  600.2 25.4 %collective-permute-start.73 = (bf16[1,256,2048]{2,1,0:T(8,128)(2,1)S(1)}, bf16[1,256,2048]{2,1,0:T(8,128)(2,1)S(1)}, u32[]{:S(2)}, u32[]{:S(2)}) collective-permute-start(bf16[1,256,2048]{2,1,0:T(8,128)(2,1)S(1)} %dynamic-slice_convert_fusion.1), channel_id=1, source_target_pairs={{0,4},{2,6},{4,0},{6,2},{1,5},{3,7},{5,1},{7,3},{8,12},{10,14},{12... | collective-permute-start | bytes 3145736 | tf_op jit(solution)/shard_map/ppermute | solution.py:68
  (169 other events, 3114.5 us)
Sparse Core Ops, SparseCore 0:
  9.6 37.1 all-gather.2
  84.7 31.7 all-gather.4
